TPU v7x, 256 devices: a whole 4x4x8 slice. The times are simulated.
256 devices in a mesh: dp: 4 (over x), expert: 64 (over z, y, core).
Axes of the slice: x: 4, y: 4, z: 8, core: 2. Of those that a mesh axis runs over, the one named last changes fastest.
Arguments:
- tokens: bfloat16 [32768, 7168], P(('dp', 'expert')), may hold values from -6 to 6
- cotangent: bfloat16 [32768, 7168], P(('dp', 'expert')), may hold values from -6 to 6
- route_ids: int32 [32768, 8], P(('dp', 'expert')), may hold values from 0 to 255, all different within a row; in each aligned block of 128 rows (0 to 127, 128 to 255, ...) at most 5 rows name the same one
- router_weights: float32 [32768, 8], P(('dp', 'expert')), may hold values from 0.05 to 0.3
- master: float32 [64, 7168, 384], P('expert', 'dp'), may hold values from -0.0625 to 0.0625
- accumulator: float32 [64, 3, 7168], P('expert', None, 'dp'), may hold values from 0.1 to 10
Outputs:
- output: bfloat16 [32768, 7168], P(('dp', 'expert'))
- input_grad: bfloat16 [32768, 7168], P(('dp', 'expert'))
- new_weights: bfloat16 [64, 7168, 384], P('expert', 'dp')
- accumulator_out: float32 [64, 3, 7168], P('expert', None, 'dp')
Inputs may be any that keep to these rules, and one draw needn't show every extreme that they name: `route_ids`: each row names distinct experts. In each aligned block of 128 rows (the rows of one device) no expert is named by more than 5 rows, a bound that some block reaches.
All inputs are finite; a program needn't handle non-finite values.
Results may differ from a plain program's by a relative error of at most 0.011.
Values may be sent and summed in bfloat16 or wider, within the bound.
No kernel may reach another device: no remote copies, remote signals or barrier semaphores. Data moves between devices by JAX's collectives and lax.ppermute only.
A program may use at most 128 MiB of HBM per device.

v0:
```python
import jax
import jax.numpy as jnp
from jax import lax
from jax.sharding import PartitionSpec as P

SLICES = 8
TOP = 8
EXP_DEV = 4


LEARN_RATE = 0.01
EPSILON = 1e-06


def from_partner(array, axis, bit):
    return lax.ppermute(array, axis, [(i, i ^ 1 << bit) for i in range(lax.axis_size(axis))])


def slot_table(block_ids, live_count, capacity):
    flat_ids = block_ids.reshape(-1)
    onehot = (flat_ids[:, None] == jnp.arange(live_count, dtype=jnp.int32)[None, :]).astype(
        jnp.int32
    )
    before = jnp.cumsum(onehot, axis=0) - onehot
    position = jnp.sum(before * onehot, axis=1)
    return jnp.where(flat_ids < live_count, flat_ids * capacity + position, live_count * capacity)


def contract_rows(left, right):
    return lax.dot_general(
        left, right, (((0,), (0,)), ((), ())), preferred_element_type=jnp.float32
    )


def contract_cols(left, right):
    return lax.dot_general(
        left, right, (((1,), (1,)), ((), ())), preferred_element_type=jnp.float32
    )


def forward_rows(in_rows, weights, slice_width):
    gate_up = jnp.dot(in_rows, weights[:, : 2 * slice_width], preferred_element_type=jnp.float32)
    gate_pre = gate_up[:, :slice_width]
    up_pre = gate_up[:, slice_width:]
    sigmoid_gate = jax.nn.sigmoid(gate_pre)
    silu_gate = gate_pre * sigmoid_gate
    hidden = (silu_gate * up_pre).astype(jnp.bfloat16)
    out_part = contract_cols(hidden, weights[:, 2 * slice_width :]).astype(jnp.bfloat16)
    return (hidden, out_part, (up_pre, sigmoid_gate, silu_gate, gate_pre))


def backward_rows(cot_rows, weights, slice_width, saved):
    up_pre, sigmoid_gate, silu_gate, gate_pre = saved
    grad_hidden = jnp.dot(
        cot_rows, weights[:, 2 * slice_width :], preferred_element_type=jnp.float32
    )
    grad_gate = grad_hidden * up_pre * sigmoid_gate * (1.0 + gate_pre * (1.0 - sigmoid_gate))
    grad_up = grad_hidden * silu_gate
    grad_pre = jnp.concatenate([grad_gate, grad_up], axis=1).astype(jnp.bfloat16)
    in_part = contract_cols(grad_pre, weights[:, : 2 * slice_width]).astype(jnp.bfloat16)
    return (grad_pre, in_part)


def local(tokens, cotangent, route_ids, router_weights, master, accumulator):
    devices_e = lax.axis_size("expert")
    live_count = devices_e // SLICES
    tok_rows = tokens.shape[0]
    model_width = tokens.shape[1]
    experts = EXP_DEV * devices_e
    capacity = max(2, 5 * tok_rows * TOP // (4 * experts))
    slice_width = master.shape[2] // 3
    quarter = master.shape[1]
    width = live_count * capacity
    own_master = master[0].astype(jnp.bfloat16)
    partner_rows = from_partner(own_master, "expert", 0)
    weights = lax.all_gather(partner_rows, "dp", axis=0, tiled=True)
    slot_ids = slot_table(route_ids, live_count, capacity)
    token_of = jnp.repeat(jnp.arange(tok_rows, dtype=jnp.int32), TOP)
    slot_token = jnp.zeros((width + 1,), jnp.int32).at[slot_ids].set(token_of)[:width]
    slot_weight = (
        jnp.zeros((width + 1,), jnp.float32).at[slot_ids].set(router_weights.reshape(-1))[:width]
    )
    filled = jnp.zeros((width + 1,), jnp.float32).at[slot_ids].set(1.0)[:width]
    token_rows = jnp.where(filled[:, None] > 0, tokens[slot_token], jnp.zeros((), jnp.bfloat16))
    grad_rows = (cotangent[slot_token].astype(jnp.float32) * slot_weight[:, None]).astype(
        jnp.bfloat16
    )

    def spread(rows):
        tiled = jnp.broadcast_to(
            rows.reshape(live_count, 1, capacity, model_width),
            (live_count, SLICES, capacity, model_width),
        )
        return tiled.reshape(devices_e, capacity, model_width)

    send_tokens = spread(token_rows)
    send_grads = spread(grad_rows)
    recv_tokens = lax.all_to_all(send_tokens, "expert", split_axis=0, concat_axis=0, tiled=True)
    in_rows = recv_tokens.reshape(-1, model_width)
    hidden, out_part, saved = forward_rows(in_rows, weights, slice_width)
    back_out = lax.all_to_all(
        out_part.reshape(devices_e, capacity, model_width),
        "expert",
        split_axis=0,
        concat_axis=0,
        tiled=True,
    )
    recv_grads = lax.all_to_all(send_grads, "expert", split_axis=0, concat_axis=0, tiled=True)
    cot_rows = recv_grads.reshape(-1, model_width)
    grad_pre, in_part = backward_rows(cot_rows, weights, slice_width, saved)
    back_in = lax.all_to_all(
        in_part.reshape(devices_e, capacity, model_width),
        "expert",
        split_axis=0,
        concat_axis=0,
        tiled=True,
    )
    grad_in = contract_rows(in_rows, grad_pre)
    grad_down = contract_rows(cot_rows, hidden)
    summed = lax.psum_scatter(
        jnp.concatenate([grad_in, grad_down], axis=1).astype(jnp.bfloat16),
        "dp",
        scatter_dimension=0,
        tiled=True,
    )
    held_grad = from_partner(summed, "expert", 0)
    slot_index = jnp.arange(width, dtype=jnp.int32)
    recv_index = jnp.arange(devices_e * capacity, dtype=jnp.int32)
    same_expert = slot_index[:, None] // capacity == recv_index[None, :] // (SLICES * capacity)
    same_place = slot_index[:, None] % capacity == recv_index[None, :] % capacity
    merge = jnp.where(same_expert & same_place, 1.0, 0.0).astype(jnp.bfloat16)
    out_sum = jnp.dot(merge, back_out.reshape(-1, model_width), preferred_element_type=jnp.float32)
    in_sum = jnp.dot(merge, back_in.reshape(-1, model_width), preferred_element_type=jnp.float32)
    pick_slots = slot_ids.reshape(tok_rows, TOP)
    hits = jnp.sum(
        (pick_slots[:, :, None] == slot_index[None, None, :]).astype(jnp.float32), axis=1
    )
    output = jnp.dot(hits * slot_weight[None, :], out_sum).astype(jnp.bfloat16)
    input_grad = jnp.dot(hits, in_sum).astype(jnp.bfloat16)
    grad_full = held_grad.astype(jnp.float32).reshape(quarter, 3, slice_width)
    mean_square = jnp.mean(grad_full * grad_full, axis=2)
    accumulator_out = accumulator[0] + mean_square.T
    scale = 1.0 / (jnp.sqrt(accumulator_out) + EPSILON)
    update = grad_full * scale.T[:, :, None]
    master_new = master[0] - LEARN_RATE * update.reshape(quarter, 3 * slice_width)
    returned = from_partner(master_new.astype(jnp.bfloat16), "expert", 0)
    return (output, input_grad, returned[None], accumulator_out[None])


def solution(mesh):
    return jax.shard_map(
        local,
        mesh=mesh,
        in_specs=(
            P(("dp", "expert"), None),
            P(("dp", "expert"), None),
            P(("dp", "expert"), None),
            P(("dp", "expert"), None),
            P("expert", "dp", None),
            P("expert", None, "dp"),
        ),
        out_specs=(
            P(("dp", "expert"), None),
            P(("dp", "expert"), None),
            P("expert", "dp", None),
            P("expert", None, "dp"),
        ),
        check_vma=False,
    )
```

profile of v0, /device:TPU:1, one launch (start us, length us, event | category | flops | bytes accessed | tf_op | source)
XLA Modules:
  0.0 768.9 jit_solution(1512021472771673495)
XLA Ops:
  12.3 4.3 scatter_custom_fusion
  16.8 4.3 scatter_custom_fusion.2
  22.5 3.9 broadcast_in_dim.79
  26.4 13.3 %all-to-all-start.2 = ((bf16[64,5,7168]{2,1,0:T(8,128)(2,1)}), bf16[64,5,7168]{2,1,0:T(8,128)(2,1)}, u32[]{:S(2)}, u32[]{:S(2)}) async-start(bf16[64,5,7168]{2,1,0:T(8,128)(2,1)} %bitcast.51), calls=%async_computation.2 | async-start | bytes 14680064 | tf_op jit(solution)/shard_map/all_to_all | solution.py:108
  46.7 4.3 scatter_custom_fusion.1
  52.5 147.6 %all-to-all-done.2 = bf16[64,5,7168]{2,1,0:T(8,128)(2,1)} async-done(((bf16[64,5,7168]{2,1,0:T(8,128)(2,1)}), bf16[64,5,7168]{2,1,0:T(8,128)(2,1)}, u32[]{:S(2)}, u32[]{:S(2)}) %all-to-all-start.2) | async-done | bytes 4587552 | tf_op jit(solution)/shard_map/all_to_all | solution.py:108
  200.0 3.8 broadcast_in_dim.78
  203.9 9.5 %all-to-all-start = ((bf16[64,5,7168]{2,1,0:T(8,128)(2,1)}), bf16[64,5,7168]{2,1,0:T(8,128)(2,1)}, u32[]{:S(2)}, u32[]{:S(2)}) async-start(bf16[64,5,7168]{2,1,0:T(8,128)(2,1)} %bitcast.52), calls=%async_computation | async-start | bytes 14680064 | tf_op jit(solution)/shard_map/all_to_all | solution.py:98
  214.1 8.3 %reshape.229 = bf16[320,7168]{1,0:T(8,128)(2,1)} reshape(bf16[64,5,7168]{2,1,0:T(8,128)(2,1)} %all-to-all-done.2) | data formatting | bytes 9175040 | tf_op jit(solution)/shard_map/reshape | solution.py:109
  222.4 151.3 %all-to-all-done = bf16[64,5,7168]{2,1,0:T(8,128)(2,1)} async-done(((bf16[64,5,7168]{2,1,0:T(8,128)(2,1)}), bf16[64,5,7168]{2,1,0:T(8,128)(2,1)}, u32[]{:S(2)}, u32[]{:S(2)}) %all-to-all-start) | async-done | bytes 4587552 | tf_op jit(solution)/shard_map/all_to_all | solution.py:98
  373.7 8.2 %reshape.225 = bf16[320,7168]{1,0:T(8,128)(2,1)} reshape(bf16[64,5,7168]{2,1,0:T(8,128)(2,1)} %all-to-all-done) | data formatting | bytes 9175040 | tf_op jit(solution)/shard_map/reshape | solution.py:99
  381.9 5.0 fusion.1
  393.1 8.0 %reshape.226 = bf16[64,5,7168]{2,1,0:T(8,128)(2,1)} reshape(bf16[320,7168]{1,0:T(8,128)(2,1)} %convolution_convert_fusion.1) | data formatting | bytes 9175040 | tf_op jit(solution)/shard_map/reshape | solution.py:102
  401.0 9.5 %all-to-all-start.1 = ((bf16[64,5,7168]{2,1,0:T(8,128)(2,1)}), bf16[64,5,7168]{2,1,0:T(8,128)(2,1)}, u32[]{:S(2)}, u32[]{:S(2)}) async-start(bf16[64,5,7168]{2,1,0:T(8,128)(2,1)} %reshape.226), calls=%async_computation.1 | async-start | bytes 14680064 | tf_op jit(solution)/shard_map/all_to_all | solution.py:101
  414.0 4.4 convolution_convert_fusion.2
  421.2 5.6 convolution_convert_fusion
  426.7 8.0 %reshape.230 = bf16[64,5,7168]{2,1,0:T(8,128)(2,1)} reshape(bf16[320,7168]{1,0:T(8,128)(2,1)} %convolution_convert_fusion) | data formatting | bytes 9175040 | tf_op jit(solution)/shard_map/reshape | solution.py:112
  434.7 136.1 %all-to-all-done.1 = bf16[64,5,7168]{2,1,0:T(8,128)(2,1)} async-done(((bf16[64,5,7168]{2,1,0:T(8,128)(2,1)}), bf16[64,5,7168]{2,1,0:T(8,128)(2,1)}, u32[]{:S(2)}, u32[]{:S(2)}) %all-to-all-start.1) | async-done | bytes 4587552 | tf_op jit(solution)/shard_map/all_to_all | solution.py:101
  570.8 9.5 %all-to-all-start.3 = ((bf16[64,5,7168]{2,1,0:T(8,128)(2,1)}), bf16[64,5,7168]{2,1,0:T(8,128)(2,1)}, u32[]{:S(2)}, u32[]{:S(2)}) async-start(bf16[64,5,7168]{2,1,0:T(8,128)(2,1)} %reshape.230), calls=%async_computation.3 | async-start | bytes 14680064 | tf_op jit(solution)/shard_map/all_to_all | solution.py:111
  590.6 8.2 %reshape.227 = bf16[320,7168]{1,0:T(8,128)(2,1)} reshape(bf16[64,5,7168]{2,1,0:T(8,128)(2,1)} %all-to-all-done.1) | data formatting | bytes 9175040 | tf_op jit(solution)/shard_map/reshape | solution.py:132
  598.8 141.8 %all-to-all-done.3 = bf16[64,5,7168]{2,1,0:T(8,128)(2,1)} async-done(((bf16[64,5,7168]{2,1,0:T(8,128)(2,1)}), bf16[64,5,7168]{2,1,0:T(8,128)(2,1)}, u32[]{:S(2)}, u32[]{:S(2)}) %all-to-all-start.3) | async-done | bytes 4587552 | tf_op jit(solution)/shard_map/all_to_all | solution.py:111
  740.6 8.2 %reshape.231 = bf16[320,7168]{1,0:T(8,128)(2,1)} reshape(bf16[64,5,7168]{2,1,0:T(8,128)(2,1)} %all-to-all-done.3) | data formatting | bytes 9175040 | tf_op jit(solution)/shard_map/reshape | solution.py:133
  748.8 5.1 convolution_convert_fusion.4
  753.9 5.0 convolution_convert_fusion.5
  (70 shorter events, 41.5 us)
Async XLA Ops:
  7.2 14.0 %copy-start = (bf16[128,7168]{1,0:T(8,128)(2,1)S(1)}, bf16[128,7168]{1,0:T(8,128)(2,1)}, u32[]{:S(2)}) copy-start(bf16[128,7168]{1,0:T(8,128)(2,1)} %param.7) | copy-start | bytes 5505028
  26.4 173.6 %all-to-all-start.2 = ((bf16[64,5,7168]{2,1,0:T(8,128)(2,1)}), bf16[64,5,7168]{2,1,0:T(8,128)(2,1)}, u32[]{:S(2)}, u32[]{:S(2)}) async-start(bf16[64,5,7168]{2,1,0:T(8,128)(2,1)} %bitcast.51), calls=%async_computation.2 | async-start | bytes 14680064 | tf_op jit(solution)/shard_map/all_to_all | solution.py:108
  39.7 11.4 %copy-start.3 = (bf16[128,7168]{1,0:T(8,128)(2,1)S(1)}, bf16[128,7168]{1,0:T(8,128)(2,1)}, u32[]{:S(2)}) copy-start(bf16[128,7168]{1,0:T(8,128)(2,1)} %param.6) | copy-start | bytes 5505028
  46.2 167.4 %collective-permute-start = (bf16[1792,384]{0,1:T(8,128)(2,1)}, bf16[1792,384]{0,1:T(8,128)(2,1)}, u32[]{:S(2)}, u32[]{:S(2)}) collective-permute-start(bf16[1792,384]{0,1:T(8,128)(2,1)} %bitcast_convert_fusion), channel_id=1, source_target_pairs={{0,1},{1,0},{2,3},{3,2},{4,5},{5,4},{6,7},{7,6},{8,9},{9,8},{10,11... | collective-permute-start | bytes 4128776 | tf_op jit(solution)/shard_map/ppermute | solution.py:16
  203.9 169.8 %all-to-all-start = ((bf16[64,5,7168]{2,1,0:T(8,128)(2,1)}), bf16[64,5,7168]{2,1,0:T(8,128)(2,1)}, u32[]{:S(2)}, u32[]{:S(2)}) async-start(bf16[64,5,7168]{2,1,0:T(8,128)(2,1)} %bitcast.52), calls=%async_computation | async-start | bytes 14680064 | tf_op jit(solution)/shard_map/all_to_all | solution.py:98
  213.4 168.5 %all-gather.2.cloned.1.call-start = ((), (), s32[]{:S(2)}) async-start(), calls=%async_computation.5 | async-start | bytes 6881280 | tf_op jit(solution)/shard_map/all_gather | solution.py:76
  381.9 5.0 copy-start.2
  381.9 6.4 copy-start.4
  401.0 169.8 %all-to-all-start.1 = ((bf16[64,5,7168]{2,1,0:T(8,128)(2,1)}), bf16[64,5,7168]{2,1,0:T(8,128)(2,1)}, u32[]{:S(2)}, u32[]{:S(2)}) async-start(bf16[64,5,7168]{2,1,0:T(8,128)(2,1)} %reshape.226), calls=%async_computation.1 | async-start | bytes 14680064 | tf_op jit(solution)/shard_map/all_to_all | solution.py:101
  410.5 169.8 %reduce-scatter.2.cloned.1.call-start = ((), (), s32[]{:S(2)}) async-start(), calls=%async_computation.6 | async-start | bytes 6881280 | tf_op jit(solution)/shard_map/reduce_scatter | solution.py:120
  570.8 169.8 %all-to-all-start.3 = ((bf16[64,5,7168]{2,1,0:T(8,128)(2,1)}), bf16[64,5,7168]{2,1,0:T(8,128)(2,1)}, u32[]{:S(2)}, u32[]{:S(2)}) async-start(bf16[64,5,7168]{2,1,0:T(8,128)(2,1)} %reshape.230), calls=%async_computation.3 | async-start | bytes 14680064 | tf_op jit(solution)/shard_map/all_to_all | solution.py:111
  580.3 7.5 copy-start.5
  580.3 3.8 collective-permute-start.1
  590.0 169.5 %collective-permute-start.2 = (bf16[1792,384]{0,1:T(8,128)(2,1)S(1)}, bf16[1792,384]{0,1:T(8,128)(2,1)}, u32[]{:S(2)}, u32[]{:S(2)}) collective-permute-start(bf16[1792,384]{0,1:T(8,128)(2,1)S(1)} %fusion.5), channel_id=1, source_target_pairs={{0,1},{1,0},{2,3},{3,2},{4,5},{5,4},{6,7},{7,6},{8,9},{9,8},{10,11... | collective-permute-start | bytes 4128776 | tf_op jit(solution)/shard_map/ppermute | solution.py:16
  748.8 13.2 %copy-start.1 = (bf16[128,7168]{1,0:T(8,128)(2,1)S(1)}, bf16[128,7168]{1,0:T(8,128)(2,1)}, u32[]{:S(2)}) copy-start(bf16[128,7168]{1,0:T(8,128)(2,1)} %param.7) | copy-start | bytes 5505028
Sparse Core Ops, SparseCore 0:
  216.0 62.5 all-gather.1
  421.3 61.0 reduce-scatter.1
where the time goes:
time: 773 us; the launch traced here: 769 us
  waiting for transfers between devices  580 us (75%)
  local copies, waits for them, and re-layouts  82.7 us (11%)
  starting transfers between devices  43.8 us (6%)
  matrix products  33.2 us (4%)
  other arithmetic  14.6 us (2%)
  between operations  14.3 us (2%)
    all_to_all x1, waiting for transfers between devices, local(): lax.all_to_all(send_tokens, 'expert', split_axis=0, concat_axis=0, tiled=...  151 us
    all_to_all x1, waiting for transfers between devices, local(): lax.all_to_all(send_grads, 'expert', split_axis=0, concat_axis=0, tiled=T...  148 us
    all_to_all x1, waiting for transfers between devices, local(): lax.all_to_all(in_part.reshape(devices_e, capacity, model_width), 'expert...  142 us
    all_to_all x1, waiting for transfers between devices, local(): lax.all_to_all(out_part.reshape(devices_e, capacity, model_width), 'exper...  136 us
  transfers between devices with their start and end apart: 9, of which 5 were waited for; matrix products, arithmetic and copies ran while one was open for 12% of the time, Pallas kernels for 0%

commit v1 on v0

v1 whole, which is shorter than its diff:
```python
import functools

import jax
import jax.numpy as jnp
from jax import lax
from jax.experimental import pallas as pl
from jax.experimental.pallas import tpu as pltpu
from jax.sharding import Mesh, PartitionSpec as P


N_X, N_Z, N_Y, N_C = 4, 8, 4, 2
CAP = 5
LEARN_RATE = 0.01
EPSILON = 1e-06
BF = jnp.bfloat16
F32 = jnp.float32
ROWS = 2 * CAP
PACK = N_X * ROWS


def swap_core(a):
    return lax.ppermute(a, "c", [(0, 1), (1, 0)])


def iota(shape, dim):
    return lax.broadcasted_iota(jnp.int32, shape, dim)


def select_kernel(ids_ref, w_ref, tok_ref, cot_ref, send_ref, tab_ref, sel_ref, row_ref, acc_ref):
    q = pl.program_id(1)
    first = (pl.program_id(0) == 0) & (q == 0)

    @pl.when(first)
    def _():
        rows = ids_ref.shape[0]
        lane = iota((rows, 128), 1)
        named = jnp.zeros((rows, 128), F32)
        weight = jnp.zeros((rows, 128), F32)
        for k in range(ids_ref.shape[1]):
            hit = ids_ref[:, k : k + 1] == lane
            named = jnp.where(hit, 1.0, named)
            weight = jnp.where(hit, w_ref[:, k : k + 1], weight)
        named_t = named.T
        weight_t = weight.T
        earlier = jnp.where(iota((rows, rows), 0) < iota((rows, rows), 1), 1.0, 0.0).astype(BF)
        place = jnp.dot(named_t.astype(BF), earlier, preferred_element_type=F32)
        code = jnp.where(named_t > 0, place + 1.0, 0.0)
        r = iota((PACK, 1), 0) % ROWS
        slot = (r % CAP + 1).astype(F32)
        is_tok = r < CAP
        for e in range(N_Z):
            block = pl.ds(e * PACK, PACK)
            picked = jnp.where(jnp.broadcast_to(code[e : e + 1, :], (PACK, rows)) == slot, 1.0, 0.0)
            weighted = picked * jnp.broadcast_to(weight_t[e : e + 1, :], (PACK, rows))
            tok_sel = jnp.where(is_tok, picked, 0.0)
            cot_sel = jnp.where(is_tok, 0.0, picked)
            sel_ref[block, :rows] = tok_sel.astype(BF)
            sel_ref[block, rows:] = cot_sel.astype(BF)
            tab_ref[block, :rows] = jnp.where(is_tok, weighted, 0.0).astype(BF)
            tab_ref[block, rows:] = cot_sel.astype(BF)
            scale = jnp.sum(weighted, axis=1, keepdims=True)
            row_ref[block, :] = jnp.broadcast_to(jnp.where(is_tok, 1.0, scale), (PACK, 128))

    @pl.when(q == 0)
    def _():
        acc_ref[...] = jnp.zeros_like(acc_ref)

    total = N_Z * PACK
    here = (iota((total, 1), 0) % PACK) // ROWS == q
    sel = jnp.where(here, sel_ref[...], jnp.zeros((), BF))
    values = jnp.concatenate([tok_ref[...], cot_ref[...]], axis=0)
    acc_ref[...] += jnp.dot(sel, values, preferred_element_type=F32)

    @pl.when(q == N_X - 1)
    def _():
        send = (acc_ref[...] * row_ref[:, :1]).astype(BF)
        send_ref[...] = send.reshape(send_ref.shape)


def select(ids, weights, tokens, cotangent):
    rows, width = tokens.shape
    seg = width // (N_X * N_C)
    total = N_Z * PACK
    return pl.pallas_call(
        select_kernel,
        grid=(N_C, N_X),
        in_specs=[
            pl.BlockSpec(ids.shape, lambda c, q: (0, 0)),
            pl.BlockSpec(weights.shape, lambda c, q: (0, 0)),
            pl.BlockSpec((rows, seg), lambda c, q: (0, q * N_C + c)),
            pl.BlockSpec((rows, seg), lambda c, q: (0, q * N_C + c)),
        ],
        out_specs=[
            pl.BlockSpec((N_Z, 1, PACK, seg), lambda c, q: (0, c, 0, 0)),
            pl.BlockSpec((total, 2 * rows), lambda c, q: (0, 0)),
        ],
        out_shape=[
            jax.ShapeDtypeStruct((N_Z, N_C, PACK, seg), BF),
            jax.ShapeDtypeStruct((total, 2 * rows), BF),
        ],
        scratch_shapes=[
            pltpu.VMEM((total, 2 * rows), BF),
            pltpu.VMEM((total, 128), F32),
            pltpu.VMEM((total, seg), F32),
        ],
        compiler_params=pltpu.CompilerParams(vmem_limit_bytes=32 << 20),
        name="select_rows",
    )(ids, weights, tokens, cotangent)


HALF = N_Z * PACK
HROWS = N_Z * CAP


def unpack_kernel(in_ref, tok_ref, cot_ref):
    q = pl.program_id(1)
    shape = (2 * HROWS, HALF)
    row, col = iota(shape, 0), iota(shape, 1)
    is_cot = (row >= HROWS).astype(jnp.int32)
    place = row - is_cot * HROWS
    want = (place // CAP) * PACK + q * ROWS + is_cot * CAP + place % CAP
    perm = jnp.where(col == want, 1.0, 0.0).astype(BF)
    out = jnp.dot(perm, in_ref[...].reshape(HALF, -1), preferred_element_type=F32).astype(BF)
    tok_ref[...] = out[:HROWS]
    cot_ref[...] = out[HROWS:]


def unpack(packed):
    seg = packed.shape[2]
    out = jax.ShapeDtypeStruct((N_C * HROWS, N_X * seg), BF)
    return pl.pallas_call(
        unpack_kernel,
        grid=(2, N_X),
        in_specs=[pl.BlockSpec((N_Z, PACK, seg), lambda h, q: (h, 0, 0))],
        out_specs=[pl.BlockSpec((HROWS, seg), lambda h, q: (h, q))] * 2,
        out_shape=[out, out],
        compiler_params=pltpu.CompilerParams(vmem_limit_bytes=32 << 20),
        name="unpack_rows",
    )(packed)


def pack_kernel(out_ref, in_ref, send_ref, acc_ref):
    q = pl.program_id(1)

    @pl.when(q == 0)
    def _():
        acc_ref[...] = jnp.zeros_like(acc_ref)

    shape = (HALF, 2 * HROWS)
    row, col = iota(shape, 0), iota(shape, 1)
    r = row % ROWS
    is_cot = (r >= CAP).astype(jnp.int32)
    want = is_cot * HROWS + (row // PACK) * CAP + r - is_cot * CAP
    hit = (col == want) & ((row % PACK) // ROWS == q)
    perm = jnp.where(hit, 1.0, 0.0).astype(BF)
    values = jnp.concatenate([out_ref[...], in_ref[...]], axis=0)
    acc_ref[...] += jnp.dot(perm, values, preferred_element_type=F32)

    @pl.when(q == N_X - 1)
    def _():
        send_ref[...] = acc_ref[...].astype(BF).reshape(send_ref.shape)


def pack(out_rows, in_rows):
    seg = out_rows.shape[1] // N_X
    return pl.pallas_call(
        pack_kernel,
        grid=(2, N_X),
        in_specs=[pl.BlockSpec((HROWS, seg), lambda h, q: (h, q))] * 2,
        out_specs=pl.BlockSpec((N_Z, PACK, seg), lambda h, q: (h, 0, 0)),
        out_shape=jax.ShapeDtypeStruct((2 * N_Z, PACK, seg), BF),
        scratch_shapes=[pltpu.VMEM((HALF, seg), F32)],
        compiler_params=pltpu.CompilerParams(vmem_limit_bytes=32 << 20),
        name="pack_rows",
    )(out_rows, in_rows)


def combine_kernel(tab_ref, back_ref, out_ref, grad_ref):
    q = pl.program_id(1)
    total = N_Z * PACK
    here = (iota((total, 1), 0) % PACK) // ROWS == q
    tab = jnp.where(here, tab_ref[...], jnp.zeros((), BF))
    merged = lax.dot_general(
        tab,
        back_ref[...].reshape(total, -1),
        (((0,), (0,)), ((), ())),
        preferred_element_type=F32,
    ).astype(BF)
    rows = out_ref.shape[0]
    out_ref[...] = merged[:rows]
    grad_ref[...] = merged[rows:]


def combine(tab, back):
    seg = back.shape[2]
    rows = tab.shape[1] // 2
    out = jax.ShapeDtypeStruct((rows, N_X * N_C * seg), BF)
    return pl.pallas_call(
        combine_kernel,
        grid=(N_C, N_X),
        in_specs=[
            pl.BlockSpec(tab.shape, lambda c, q: (0, 0)),
            pl.BlockSpec((N_Z, 1, PACK, seg), lambda c, q: (0, c, 0, 0)),
        ],
        out_specs=[pl.BlockSpec((rows, seg), lambda c, q: (0, q * N_C + c))] * 2,
        out_shape=[out, out],
        compiler_params=pltpu.CompilerParams(vmem_limit_bytes=32 << 20),
        name="combine_rows",
    )(tab, back.reshape(N_Z, N_C, PACK, seg))


def dot_nn(a, b):
    return jnp.dot(a, b, preferred_element_type=F32)


def dot_nt(a, b):
    return lax.dot_general(a, b, (((1,), (1,)), ((), ())), preferred_element_type=F32)


def dot_tn(a, b):
    return lax.dot_general(a, b, (((0,), (0,)), ((), ())), preferred_element_type=F32)


def gather_y(rows):
    return lax.all_gather(rows, "y", axis=0, tiled=True)


def scatter_y(rows):
    return lax.psum_scatter(rows, "y", scatter_dimension=0, tiled=True)


def exchange(blocks):
    return lax.all_to_all(blocks, ("z", "c"), split_axis=0, concat_axis=0, tiled=True)


def local(tokens, cotangent, route_ids, router_weights, master, accumulator):
    quarter, cols = master.shape[1], master.shape[2]
    hid = cols // 3
    seg = quarter // N_C
    core = lax.axis_index("c")

    mine = master[0].astype(BF)
    keep = lax.dynamic_slice_in_dim(mine, core * seg, seg, 0)
    give = lax.dynamic_slice_in_dim(mine, (1 - core) * seg, seg, 0)
    pair = jnp.concatenate([keep, swap_core(give)], axis=1)
    weights = lax.all_gather(pair, "x", axis=0, tiled=True)

    send, tab = select(route_ids, router_weights, tokens, cotangent)
    packed = exchange(send.reshape(N_Z * N_C, PACK, seg))
    tok_part, cot_part = unpack(packed)
    in_rows = gather_y(tok_part)
    cot_rows = gather_y(cot_part)

    gate_up = jnp.concatenate([weights[:, : 2 * hid], weights[:, cols : cols + 2 * hid]], axis=1)
    down = jnp.concatenate([weights[:, 2 * hid : cols], weights[:, cols + 2 * hid :]], axis=1)
    pre_half = dot_nn(in_rows, gate_up)
    grad_half = dot_nn(cot_rows, down)

    def sum_cores(half):
        other = swap_core(half)
        mid = half.shape[1] // 2
        return half + jnp.concatenate([other[:, mid:], other[:, :mid]], axis=1)

    pre = sum_cores(pre_half).reshape(-1, 2, 2, hid)
    grad_hidden = sum_cores(grad_half).reshape(-1, 2, hid)
    gate_pre, up_pre = pre[:, :, 0], pre[:, :, 1]
    sig = jax.nn.sigmoid(gate_pre)
    silu = gate_pre * sig
    hidden = (silu * up_pre).astype(BF)
    grad_gate = grad_hidden * up_pre * sig * (1.0 + gate_pre * (1.0 - sig))
    grad_up = grad_hidden * silu
    grad_pre = jnp.stack([grad_gate, grad_up], axis=2).astype(BF)
    hidden = hidden.reshape(-1, 2 * hid)
    grad_pre = grad_pre.reshape(-1, 4 * hid)

    out_part = dot_nt(hidden, down).astype(BF)
    in_part = dot_nt(grad_pre, gate_up).astype(BF)
    back = exchange(pack(scatter_y(out_part), scatter_y(in_part)))
    output, input_grad = combine(tab, back)

    grad_gu = dot_tn(in_rows, grad_pre).astype(BF)
    grad_dn = dot_tn(cot_rows, hidden).astype(BF)
    full = jnp.concatenate(
        [grad_gu[:, : 2 * hid], grad_dn[:, :hid], grad_gu[:, 2 * hid :], grad_dn[:, hid:]], axis=1
    )
    summed = lax.psum_scatter(full, "x", scatter_dimension=0, tiled=True)
    here, there = summed[:, :cols], swap_core(summed[:, cols:])
    grad = jnp.where(
        core == 0,
        jnp.concatenate([here, there], axis=0),
        jnp.concatenate([there, here], axis=0),
    )
    grad = grad.astype(F32).reshape(quarter, 3, hid)
    accumulator_out = accumulator[0] + jnp.mean(grad * grad, axis=2).T
    scale = 1.0 / (jnp.sqrt(accumulator_out) + EPSILON)
    update = grad * scale.T[:, :, None]
    master_new = master[0] - LEARN_RATE * update.reshape(quarter, cols)
    returned = swap_core(master_new.astype(BF))
    return output, input_grad, returned[None], accumulator_out[None]


def solution(mesh):
    fine = Mesh(mesh.devices.reshape(N_X, N_Z, N_Y, N_C), ("x", "z", "y", "c"))
    rows = P(("x", "z", "y", "c"), None)
    weights = P(("z", "y", "c"), "x", None)
    sums = P(("z", "y", "c"), None, "x")
    return jax.shard_map(
        local,
        mesh=fine,
        in_specs=(rows, rows, rows, rows, weights, sums),
        out_specs=(rows, rows, weights, sums),
        check_vma=False,
    )
```

time: 773 us -> 389 us (0.50)
  waiting for transfers between devices: 580 us -> 229 us
  local copies, waits for them, and re-layouts: 82.7 us -> 33.4 us
  blocking collectives: 0 us -> 37.7 us
  starting transfers between devices: 43.8 us -> 13.7 us
  Pallas kernels: 0 us -> 20.8 us
  matrix products: 33.2 us -> 20.6 us
    all_to_all x4 -> x1, waiting for transfers between devices: 577 us -> 25.4 us  [exchange(): lax.all_to_all(blocks, ('z', 'c'), split_axis=0, concat_axis=0, tiled=True)]
    all_gather x1 -> x3, waiting for transfers between devices: 0.01 us -> 81.3 us  [the longest x2 68 us: gather_y(): return lax.all_gather(rows, 'y', axis=0, tiled=True)]
    reduce_scatter x1 -> x2, waiting for transfers between devices: 0.02 us -> 69.1 us  [scatter_y(): return lax.psum_scatter(rows, 'y', scatter_dimension=0, tiled=True)]
    unnamed x2 -> x7, waiting for transfers between devices: 0.51 us -> 51.2 us
    reshape x8 -> x2, local copies, waits for them, and re-layouts: 49 us -> 1.32 us  [the longest x1 0.9 us: local(): grad_hidden = sum_cores(grad_half).reshape(-1, 2, hid)]
    all_to_all x0 -> x1, blocking collectives: none -> 37.7 us  [exchange(): lax.all_to_all(blocks, ('z', 'c'), split_axis=0, concat_axis=0, tiled=True)]
    all_to_all x4 -> x1, starting transfers between devices: 41.8 us -> 7.8 us  [exchange(): lax.all_to_all(blocks, ('z', 'c'), split_axis=0, concat_axis=0, tiled=True)]
    pallas_call x0 -> x4, Pallas kernels: none -> 20.8 us  [the longest x1 6.22 us: combine(): pl.pallas_call(combine_kernel, grid=(N_C, N_X), in_specs=[pl.BlockSpec(ta...]
  transfers between devices with their start and end apart: 9 -> 12, of which waited for: 5 -> 8; matrix products, arithmetic and copies ran while one was open for 12% -> 8% of each run, Pallas kernels for 0% -> 5%
where the time goes in v1:
time: 389 us; the launch traced here: 388 us
  waiting for transfers between devices  229 us (59%)
  blocking collectives  37.7 us (10%)
  local copies, waits for them, and re-layouts  33.4 us (9%)
  Pallas kernels  20.8 us (5%)
  matrix products  20.6 us (5%)
  other arithmetic  18.7 us (5%)
  between operations  14.3 us (4%)
  starting transfers between devices  13.7 us (4%)
    reduce_scatter x2, waiting for transfers between devices, scatter_y(): return lax.psum_scatter(rows, 'y', scatter_dimension=0, tiled=True)  69.1 us
    all_gather x2, waiting for transfers between devices, gather_y(): return lax.all_gather(rows, 'y', axis=0, tiled=True)  68 us
    unnamed x7, waiting for transfers between devices  51.2 us
    all_to_all x1, blocking collectives, exchange(): lax.all_to_all(blocks, ('z', 'c'), split_axis=0, concat_axis=0, tiled=True)  37.7 us
    all_to_all x1, waiting for transfers between devices, exchange(): lax.all_to_all(blocks, ('z', 'c'), split_axis=0, concat_axis=0, tiled=True)  25.4 us
    unnamed x35, local copies, waits for them, and re-layouts  20.7 us
    all_gather x1, waiting for transfers between devices, local(): weights = lax.all_gather(pair, 'x', axis=0, tiled=True)  13.4 us
    concatenate x1, other arithmetic, local(): jnp.concatenate([grad_gu[:, :2 * hid], grad_dn[:, :hid], grad_gu[:, 2 * h...  8.78 us
  transfers between devices with their start and end apart: 12, of which 8 were waited for; matrix products, arithmetic and copies ran while one was open for 8% of the time, Pallas kernels for 5%

profile of v1, /device:TPU:1, one launch (start us, length us, event | category | flops | bytes accessed | tf_op | source)
XLA Modules:
  0.0 388.1 jit_solution(14594593749381008276)
XLA Ops:
  7.2 2.2 copy.28
  13.0 3.3 collective-permute-start
  21.1 5.1 %select_rows.1 = (bf16[8,2,40,896]{3,2,1,0:T(8,128)(2,1)S(1)}, bf16[320,256]{1,0:T(8,128)(2,1)S(1)}) custom-call(s32[128,8]{1,0:T(8,128)S(1)} %copy.26.ids_ref, f32[128,8]{1,0:T(8,128)S(1)} %copy.27.w_ref, bf16[128,7168]{1,0:T(8,128)(2,1)S(1)} %copy-done, bf16[128,7168]{1,0:T(8,128)(2,1)S(1)} %copy-done.1), custom_call_target="tpu_custom_call" | custom-call | tf_op jit(solution)/shard_map/select_rows/pallas_call | solution.py:84
  26.2 37.7 %all_to_all.10.in_ref = bf16[16,40,896]{2,1,0:T(8,128)(2,1)S(1)} all-to-all(bf16[16,40,896]{2,1,0:T(8,128)(2,1)S(1)} %bitcast.55), channel_id=1, replica_groups=mesh['x'=4,'z'=8,'y'=4,'c'=2] {'z','c'}, dimensions={0} | all-to-all | bytes 2293760 | tf_op jit(solution)/shard_map/all_to_all | solution.py:233
  63.9 3.9 %unpack_rows.1 = (bf16[80,3584]{1,0:T(8,128)(2,1)}, bf16[80,3584]{1,0:T(8,128)(2,1)}) custom-call(bf16[16,40,896]{2,1,0:T(8,128)(2,1)S(1)} %all_to_all.10.in_ref), custom_call_target="tpu_custom_call" | custom-call | tf_op jit(solution)/shard_map/unpack_rows/pallas_call | solution.py:131
  68.6 13.4 %all-gather.6.cloned.1.call-done = bf16[3584,768]{0,1:T(8,128)(2,1)} async-done(((bf16[896,768]{0,1:T(8,128)(2,1)}), bf16[3584,768]{0,1:T(8,128)(2,1)}) %all-gather.6.cloned.1.call-update) | async-done | bytes 5505040 | tf_op jit(solution)/shard_map/all_gather | solution.py:246
  83.6 36.5 %all-gather.8.cloned.1.call-done = bf16[320,3584]{1,0:T(8,128)(2,1)} async-done(((bf16[80,3584]{1,0:T(8,128)(2,1)}), bf16[320,3584]{1,0:T(8,128)(2,1)}) %all-gather.8.cloned.1.call-update) | async-done | bytes 2293776 | tf_op jit(solution)/shard_map/all_gather | solution.py:225
  120.1 3.3 fusion.4
  125.6 31.5 %all-gather.4.cloned.1.call-done = bf16[320,3584]{1,0:T(8,128)(2,1)} async-done(((bf16[80,3584]{1,0:T(8,128)(2,1)}), bf16[320,3584]{1,0:T(8,128)(2,1)}) %all-gather.4.cloned.1.call-update) | async-done | bytes 2293776 | tf_op jit(solution)/shard_map/all_gather | solution.py:225
  157.0 4.4 %fusion.3 = f32[320,512]{1,0:T(8,128)} fusion(bf16[320,3584]{1,0:T(8,128)(2,1)} %all-gather.4.cloned.1.call-done, bf16[3584,256]{0,1:T(8,128)(2,1)} %get-tuple-element.39, bf16[3584,256]{0,1:T(8,128)(2,1)S(1)} %get-tuple-element.38), kind=kOutput, calls=%fused_computation.12 | convolution fusion | flops 1181745152 | bytes 6619136 | tf_op jit(solution)/shard_map/dot_general | solution.py:213
  166.7 2.9 slice_reduce_fusion.1
  171.4 2.8 convolution_convert_fusion.3
  178.3 8.8 %pad_maximum_fusion = bf16[3584,768]{0,1:T(8,128)(2,1)} fusion(bf16[3584,128]{0,1:T(8,128)(2,1)S(1)} %get-tuple-element.43, bf16[3584,256]{0,1:T(8,128)(2,1)S(1)} %get-tuple-element.41, bf16[3584,128]{0,1:T(8,128)(2,1)S(1)} %get-tuple-element.42, bf16[3584,256]{0,1:T(8,128)(2,1)S(1)} %get-tuple-element.40), kind=kLoop, calls=%fused_computation.1 | loop fusion | flops 22020096 | bytes 11010048 | tf_op jit(solution)/shard_map/concatenate | solution.py:283
  187.1 8.3 %copy.37 = bf16[3584,768]{1,0:T(8,128)(2,1)} copy(bf16[3584,768]{0,1:T(8,128)(2,1)} %pad_maximum_fusion) | data formatting | bytes 11010048
  196.6 3.6 convolution_convert_fusion.2
  200.4 4.3 %convolution_convert_fusion.1 = bf16[320,3584]{1,0:T(8,128)(2,1)} fusion(bf16[320,512]{1,0:T(8,128)(2,1)S(1)} %convert_element_type.37, bf16[3584,256]{0,1:T(8,128)(2,1)} %get-tuple-element.39, bf16[3584,256]{0,1:T(8,128)(2,1)S(1)} %get-tuple-element.38), kind=kOutput, calls=%fused_computation.2 | convolution fusion | flops 1182892032 | bytes 6291456 | tf_op jit(solution)/shard_map/dot_general | solution.py:217
  204.8 50.4 %reduce-scatter.10.cloned.1.call-done = bf16[896,768]{1,0:T(8,128)(2,1)} async-done(((bf16[3584,768]{1,0:T(8,128)(2,1)}), bf16[896,768]{1,0:T(8,128)(2,1)}) %reduce-scatter.10.cloned.1.call-update) | async-done | bytes 1376272
  258.4 32.9 %reduce-scatter.6.cloned.1.call-done.out_ref = bf16[80,3584]{1,0:T(8,128)(2,1)} async-done(((bf16[320,3584]{1,0:T(8,128)(2,1)}), bf16[80,3584]{1,0:T(8,128)(2,1)}) %reduce-scatter.6.cloned.1.call-update) | async-done | bytes 573456 | tf_op jit(solution)/shard_map/reduce_scatter | solution.py:229
  291.3 36.2 %reduce-scatter.8.cloned.1.call-done.in_ref = bf16[80,3584]{1,0:T(8,128)(2,1)} async-done(((bf16[320,3584]{1,0:T(8,128)(2,1)}), bf16[80,3584]{1,0:T(8,128)(2,1)}) %reduce-scatter.8.cloned.1.call-update) | async-done | bytes 573456 | tf_op jit(solution)/shard_map/reduce_scatter | solution.py:229
  329.6 5.6 %pack_rows.1 = bf16[16,40,896]{2,1,0:T(8,128)(2,1)} custom-call(bf16[80,3584]{1,0:T(8,128)(2,1)S(1)} %copy-done.2, bf16[80,3584]{1,0:T(8,128)(2,1)S(1)} %copy-done.3), custom_call_target="tpu_custom_call" | custom-call | tf_op jit(solution)/shard_map/pack_rows/pallas_call | solution.py:166
  335.2 7.8 %all-to-all-start.1 = ((bf16[16,40,896]{2,1,0:T(8,128)(2,1)}), bf16[16,40,896]{2,1,0:T(8,128)(2,1)S(1)}, u32[]{:S(2)}, u32[]{:S(2)}) async-start(bf16[16,40,896]{2,1,0:T(8,128)(2,1)} %pack_rows.1), calls=%async_computation.3 | async-start | bytes 2293760 | tf_op jit(solution)/shard_map/all_to_all | solution.py:233
  343.9 3.5 fusion.2
  347.5 25.4 %all-to-all-done.1 = bf16[16,40,896]{2,1,0:T(8,128)(2,1)S(1)} async-done(((bf16[16,40,896]{2,1,0:T(8,128)(2,1)}), bf16[16,40,896]{2,1,0:T(8,128)(2,1)S(1)}, u32[]{:S(2)}, u32[]{:S(2)}) %all-to-all-start.1) | async-done | bytes 1146912 | tf_op jit(solution)/shard_map/all_to_all | solution.py:233
  372.9 6.2 %combine_rows.1 = (bf16[128,7168]{1,0:T(8,128)(2,1)}, bf16[128,7168]{1,0:T(8,128)(2,1)}) custom-call(bf16[320,256]{1,0:T(8,128)(2,1)S(1)} %get-tuple-element.10.tab_ref, bf16[8,2,40,896]{3,2,1,0:T(8,128)(2,1)S(1)} %bitcast.54), custom_call_target="tpu_custom_call" | custom-call | tf_op jit(solution)/shard_map/combine_rows/pallas_call | solution.py:198
  (76 shorter events, 33.6 us)
Async XLA Ops:
  7.2 74.9 %all-gather.6.cloned.1.call-start = ((), (), s32[]{:S(2)}) async-start(), calls=%async_computation.6 | async-start | bytes 6881280 | tf_op jit(solution)/shard_map/all_gather | solution.py:246
  9.5 2.1 copy-start.4
  12.9 6.4 %copy-start.11 = (s32[128,8]{0,1:T(8,128)S(1)}, s32[128,8]{0,1:T(8,128)}, u32[]{:S(2)}) copy-start(s32[128,8]{0,1:T(8,128)} %param.8) | copy-start | bytes 12292
  12.9 6.5 %copy-start.12 = (f32[128,8]{0,1:T(8,128)S(1)}, f32[128,8]{0,1:T(8,128)}, u32[]{:S(2)}) copy-start(f32[128,8]{0,1:T(8,128)} %param.9) | copy-start | bytes 12292
  13.0 6.6 %copy-start = (bf16[128,7168]{1,0:T(8,128)(2,1)S(1)}, bf16[128,7168]{1,0:T(8,128)(2,1)}, u32[]{:S(2)}) copy-start(bf16[128,7168]{1,0:T(8,128)(2,1)} %tok_ref.1) | copy-start | bytes 5505028
  13.0 5.1 %collective-permute-start = (bf16[896,384]{0,1:T(8,128)(2,1)S(1)}, bf16[896,384]{0,1:T(8,128)(2,1)S(1)}, u32[]{:S(2)}, u32[]{:S(2)}) collective-permute-start(bf16[896,384]{0,1:T(8,128)(2,1)S(1)} %get-tuple-element.47), channel_id=1, source_target_pairs={{0,1},{1,0},{2,3},{3,2},{4,5},{5,4},{6,7},{7,6},{8,9},{9,8},{10,11... | collective-permute-start | bytes 2064392 | tf_op jit(solution)/shard_map/ppermute | solution.py:22
  19.3 100.8 %all-gather.8.cloned.1.call-start = ((), (), s32[]{:S(2)}) async-start(), calls=%async_computation.8 | async-start | bytes 2867200 | tf_op jit(solution)/shard_map/all_gather | solution.py:225
  19.5 1.5 copy-start.1
  67.9 89.2 %all-gather.4.cloned.1.call-start = ((), (), s32[]{:S(2)}) async-start(), calls=%async_computation.5 | async-start | bytes 2867200 | tf_op jit(solution)/shard_map/all_gather | solution.py:225
  68.6 186.6 %reduce-scatter.10.cloned.1.call-start = ((), (), s32[]{:S(2)}) async-start(), calls=%async_computation.10 | async-start | bytes 6881280
  83.6 39.8 %copy-start.6 = (bf16[3584,128]{0,1:T(8,128)(2,1)}, bf16[3584,128]{0,1:T(8,128)(2,1)S(1)}, u32[]{:S(2)}) copy-start(bf16[3584,128]{0,1:T(8,128)(2,1)S(1)} %get-tuple-element.36) | copy-start | bytes 2752516
  83.6 39.8 %copy-start.8 = (bf16[3584,128]{0,1:T(8,128)(2,1)}, bf16[3584,128]{0,1:T(8,128)(2,1)S(1)}, u32[]{:S(2)}) copy-start(bf16[3584,128]{0,1:T(8,128)(2,1)S(1)} %get-tuple-element.37) | copy-start | bytes 2752516
  120.1 4.0 %copy-start.5 = (bf16[3584,768]{0,1:T(8,128)(2,1)S(1)}, bf16[3584,768]{0,1:T(8,128)(2,1)}, u32[]{:S(2)}) copy-start(bf16[3584,768]{0,1:T(8,128)(2,1)} %all-gather.6.cloned.1.call-done) | copy-start | bytes 16515076
  123.4 38.7 %collective-permute-start.2 = (f32[320,256]{1,0:T(8,128)}, f32[320,256]{1,0:T(8,128)}, u32[]{:S(2)}, u32[]{:S(2)}) collective-permute-start(f32[320,256]{1,0:T(8,128)} %fusion.4), channel_id=1, source_target_pairs={{0,1},{1,0},{2,3},{3,2},{4,5},{5,4},{6,7},{7,6},{8,9},{9,8},{10,11... | collective-permute-start | bytes 983048 | tf_op jit(solution)/shard_map/ppermute | solution.py:22
  161.5 3.6 collective-permute-start.1
  169.7 1.7 copy-start.9
  174.2 1.6 copy-start.13
  195.4 1.2 copy-start.7
  195.4 95.9 %reduce-scatter.6.cloned.1.call-start = ((), (), s32[]{:S(2)}) async-start(), calls=%async_computation.7 | async-start | bytes 2867200 | tf_op jit(solution)/shard_map/reduce_scatter | solution.py:229
  200.2 127.4 %reduce-scatter.8.cloned.1.call-start = ((), (), s32[]{:S(2)}) async-start(), calls=%async_computation.9 | async-start | bytes 2867200 | tf_op jit(solution)/shard_map/reduce_scatter | solution.py:229
  257.8 85.6 %collective-permute-start.3 = (bf16[896,384]{0,1:T(8,128)(2,1)}, bf16[896,384]{0,1:T(8,128)(2,1)S(1)}, u32[]{:S(2)}, u32[]{:S(2)}) collective-permute-start(bf16[896,384]{0,1:T(8,128)(2,1)} %copy.43), channel_id=1, source_target_pairs={{0,1},{1,0},{2,3},{3,2},{4,5},{5,4},{6,7},{7,6},{8,9},{9,8},{10,11... | collective-permute-start | bytes 2064392 | tf_op jit(solution)/shard_map/ppermute | solution.py:22
  335.2 8.7 %copy-start.10 = (f32[1,3,1792]{2,0,1:T(1,128)S(1)}, f32[1,3,1792]{2,0,1:T(1,128)}, u32[]{:S(2)}) copy-start(f32[1,3,1792]{2,0,1:T(1,128)} %param.11) | copy-start | bytes 64516
  335.2 37.7 %all-to-all-start.1 = ((bf16[16,40,896]{2,1,0:T(8,128)(2,1)}), bf16[16,40,896]{2,1,0:T(8,128)(2,1)S(1)}, u32[]{:S(2)}, u32[]{:S(2)}) async-start(bf16[16,40,896]{2,1,0:T(8,128)(2,1)} %pack_rows.1), calls=%async_computation.3 | async-start | bytes 2293760 | tf_op jit(solution)/shard_map/all_to_all | solution.py:233
  347.4 32.4 %collective-permute-start.4 = (bf16[1792,384]{0,1:T(8,128)(2,1)}, bf16[1792,384]{0,1:T(8,128)(2,1)S(1)}, u32[]{:S(2)}, u32[]{:S(2)}) collective-permute-start(bf16[1792,384]{0,1:T(8,128)(2,1)} %fusion.2), channel_id=1, source_target_pairs={{0,1},{1,0},{2,3},{3,2},{4,5},{5,4},{6,7},{7,6},{8,9},{9,8},{10,11... | collective-permute-start | bytes 4128776 | tf_op jit(solution)/shard_map/ppermute | solution.py:22
  (2 other events, 2.1 us)
Sparse Core Ops, SparseCore 0:
  19.4 62.5 all-gather.5
  84.4 35.6 all-gather.7
  121.9 35.0 all-gather.3
  195.5 59.6 reduce-scatter.9
  257.6 33.6 reduce-scatter.5
  293.9 33.5 reduce-scatter.7
